TPU v7x, 256 devices: a whole 4x4x8 slice. The times are simulated.
256 devices in a mesh: prefix: 8 (over z), feat: 32 (over y, x, core).
Axes of the slice: x: 4, y: 4, z: 8, core: 2. Of those that a mesh axis runs over, the one named last changes fastest.
Arguments:
- activations: float32 [1024, 1152], P('feat'), may hold values from -6 to 6
- enc_weight: float32 [16, 9216, 1152], P('prefix', 'feat'), may hold values from -0.1875 to 0.1875
- dec_weight: float32 [16, 9216, 1152], P('prefix', 'feat'), may hold values from -0.0625 to 0.0625
Outputs:
- enc_grad: float32 [16, 9216, 1152], P('prefix', 'feat')
- dec_grad: float32 [16, 9216, 1152], P('prefix', 'feat')
All inputs are finite; a program needn't handle non-finite values.
Results may differ from a plain program's by a relative error of at most 0.000094.
Values sent between devices are 32-bit elements; how exact they have to be, the bound alone decides.
No kernel may reach another device: no remote copies, remote signals or barrier semaphores. Data moves between devices by JAX's collectives and lax.ppermute only.
A program may use at most 128 MiB of HBM per device.

v0:
```python
import jax
import jax.numpy as jnp
from jax import lax
from jax.sharding import PartitionSpec as P

HIGHEST = lax.Precision.HIGHEST


def entering(shard, axis, combine, identity, reverse):
    count, here = (lax.axis_size(axis), lax.axis_index(axis))
    everything = lax.all_gather(shard, axis)
    start = jnp.broadcast_to(jnp.asarray(identity, shard.dtype), shard.shape)

    def step(k, before):
        at = count - 1 - k if reverse else k
        reached = at > here if reverse else at < here
        new = combine(before, everything[at])
        return jnp.where(reached, new, before)

    return lax.fori_loop(0, count, step, start)


def add_terms(earlier, later):
    return earlier + later


def chain_scan(decoded, act_rows):
    group_total = jnp.sum(decoded, axis=1)
    nothing = jnp.zeros_like(group_total)
    before = entering(group_total, "prefix", add_terms, nothing, False)
    rebuilt = before[:, None, :] + jnp.cumsum(decoded, axis=1)
    errors = rebuilt - act_rows[:, None, :]
    error_total = jnp.sum(errors, axis=1)
    beyond = entering(error_total, "prefix", add_terms, nothing, True)
    return beyond[:, None, :] + jnp.flip(jnp.cumsum(jnp.flip(errors, 1), axis=1), 1)


def per_device(activations, enc_weight, dec_weight):
    local_groups, local_feats, model_width = enc_weight.shape
    gathered = lax.all_gather(activations, "feat", axis=0, tiled=True)
    tokens = gathered.shape[0]
    pre_act = jnp.einsum("nd,gkd->gnk", gathered, enc_weight, precision=HIGHEST)
    features = jax.nn.softplus(4.0 * pre_act) / 4.0
    slopes = jax.nn.sigmoid(4.0 * pre_act)
    factor = 2.0 / tokens
    empty = jnp.zeros(enc_weight.shape, jnp.float32)
    own_rows = tokens // lax.axis_size("feat")
    feat_rows = features
    product = jnp.einsum("gnk,gkd->ngd", feat_rows, dec_weight, precision=HIGHEST)
    summed = lax.psum_scatter(
        product.reshape(lax.axis_size("feat") * own_rows, local_groups * model_width),
        "feat",
        scatter_dimension=0,
        tiled=True,
    )
    decoded = summed.reshape(summed.shape[0], local_groups, model_width)
    suffix = factor * chain_scan(decoded, activations)
    suffix_piece = lax.all_gather(suffix, "feat", axis=0, tiled=True)
    feat_rows = features
    dec_new = empty + jnp.einsum("gnk,ngd->gkd", feat_rows, suffix_piece, precision=HIGHEST)
    gate = jnp.einsum("ngd,gkd->gnk", suffix_piece, dec_weight, precision=HIGHEST) * slopes
    enc_new = empty + jnp.einsum("gnk,nd->gkd", gate, gathered, precision=HIGHEST)
    return (enc_new, dec_new)


def solution(mesh):
    in_specs = (P("feat", None), P("prefix", "feat", None), P("prefix", "feat", None))
    out_specs = (P("prefix", "feat", None), P("prefix", "feat", None))
    return jax.shard_map(
        per_device, mesh=mesh, in_specs=in_specs, out_specs=out_specs, check_vma=False
    )
```

profile of v0, /device:TPU:1, one launch (start us, length us, event | category | flops | bytes accessed | tf_op | source)
XLA Modules:
  0.0 425.4 jit_solution(15453496965193077454)
XLA Ops:
  8.0 58.4 %all-gather.7.cloned.1.call-done = f32[1024,1152]{1,0:T(8,128)} async-done(((f32[32,1152]{1,0:T(8,128)}), f32[1024,1152]{1,0:T(8,128)}) %all-gather.7.cloned.1.call-update) | async-done | bytes 4718608 | tf_op jit(solution)/shard_map/all_gather | solution.py:40
  66.4 12.5 %fusion.2 = f32[2,288,1024]{2,1,0:T(8,128)S(1)} fusion(f32[2,288,1152]{2,1,0:T(8,128)} %param.8, f32[1024,1152]{1,0:T(8,128)} %all-gather.7.cloned.1.call-done), kind=kOutput, calls=%fused_computation.6 | convolution fusion | flops 8153726976 | bytes 9732096 | tf_op jit(solution)/shard_map/nd,gkd->gnk/dot_general | solution.py:42
  78.9 1.4 copy-done.2
  80.3 19.8 %convolution_bitcast_fusion = f32[1024,2,1152]{2,0,1:T(8,128)} fusion(f32[2,288,1152]{2,1,0:T(8,128)S(1)} %copy-done, f32[2,288,1024]{2,1,0:T(8,128)S(1)} %fusion.2), kind=kOutput, calls=%fused_computation.3 | convolution fusion | flops 8158445568 | bytes 14450688 | tf_op jit(solution)/shard_map/gnk,gkd->ngd/dot_general | solution.py:49
  100.1 9.6 %copy.8 = f32[1024,2,1152]{0,2,1:T(8,128)} copy(f32[1024,2,1152]{2,0,1:T(8,128)} %convolution_bitcast_fusion) | data formatting | bytes 18874368 | tf_op jit(solution)/shard_map/gnk,gkd->ngd/transpose | solution.py:49
  109.8 9.6 %copy.13 = f32[1024,2304]{1,0:T(8,128)} copy(f32[1024,2304]{0,1:T(8,128)} %bitcast.55) | data formatting | bytes 18874368
  119.5 100.5 %reduce-scatter.4.cloned.1.call-done = f32[32,2304]{1,0:T(8,128)} async-done(((f32[1024,2304]{1,0:T(8,128)}), f32[32,2304]{1,0:T(8,128)}) %reduce-scatter.4.cloned.1.call-update) | async-done | bytes 294928
  219.9 2.3 copy.14
  222.3 1.4 reduce_sum.18
  224.7 1.6 copy.10
  226.3 33.4 %all-gather.11.cloned.1.call-done = f32[256,1152]{1,0:T(8,128)} async-done(((f32[32,1152]{1,0:T(8,128)}), f32[256,1152]{1,0:T(8,128)}) %all-gather.11.cloned.1.call-update) | async-done | bytes 1179664 | tf_op jit(solution)/shard_map/all_gather | solution.py:11
  259.7 7.8 %while.30 = (s32[]{:T(128)}, f32[32,1152]{1,0:T(8,128)S(1)}, s32[]{:T(128)}, f32[8,32,1152]{2,1,0:T(8,128)}, s32[]{:T(128)}, /*index=5*/s32[]{:T(128)}) while((s32[]{:T(128)}, f32[32,1152]{1,0:T(8,128)S(1)}, s32[]{:T(128)}, f32[8,32,1152]{2,1,0:T(8,128)}, s32[]{:T(128)}, /*index=5*/s32[]{:T(128)}) %tuple.89), condition=%wide.region_3.4_spmd.clone, body=%wide.region_2.3_spmd.clone.sunk | while | flops 110596 | bytes 442461 | solution.py:20
  260.7 1.0 add_select_fusion.4
  261.7 1.0 add_select_fusion.4
  262.6 1.0 add_select_fusion.4
  263.6 1.0 add_select_fusion.4
  264.6 1.0 add_select_fusion.4
  265.6 1.0 add_select_fusion.4
  266.6 1.0 add_select_fusion.4
  268.6 12.6 %fusion.30 = f32[32,2,1152]{2,0,1:T(8,128)S(1)} fusion(f32[32,2,1152]{2,0,1:T(8,128)S(1)} %rev.7), kind=kOutput, calls=%fused_computation.36 | output fusion | flops 73728 | bytes 589824 | tf_op jit(solution)/shard_map/jit(cumsum)/reduce_window_sum | solution.py:35
  281.1 24.7 %all-gather.13.cloned.1.call-done = f32[256,1152]{1,0:T(8,128)} async-done(((f32[32,1152]{1,0:T(8,128)}), f32[256,1152]{1,0:T(8,128)}) %all-gather.13.cloned.1.call-update) | async-done | bytes 1179664 | tf_op jit(solution)/shard_map/all_gather | solution.py:11
  305.9 7.9 %while.31 = (s32[]{:T(128)}, f32[32,1152]{1,0:T(8,128)S(1)}, s32[]{:T(128)}, f32[8,32,1152]{2,1,0:T(8,128)}, s32[]{:T(128)}, /*index=5*/s32[]{:T(128)}, s32[]{:T(128)}, s32[]{:T(128)}) while((s32[]{:T(128)}, f32[32,1152]{1,0:T(8,128)S(1)}, s32[]{:T(128)}, f32[8,32,1152]{2,1,0:T(8,128)}, s32[]{:T(128)}, /*index=5*/s32[]{:T(128)}, ...), condition=%wide.region_7.8_spmd.clone, body=%wide.region_6.7_spmd.clone.sunk | while | flops 110600 | bytes 442523 | solution.py:20
  306.8 1.0 add_select_fusion.5
  307.8 1.0 add_select_fusion.5
  308.8 1.0 add_select_fusion.5
  309.8 1.0 add_select_fusion.5
  310.8 1.0 add_select_fusion.5
  312.8 1.0 add_select_fusion.5
  314.5 64.2 %all-gather.9.cloned.1.call-done = f32[1024,2,1152]{2,0,1:T(8,128)} async-done(((f32[32,2,1152]{2,0,1:T(8,128)}), f32[1024,2,1152]{2,0,1:T(8,128)}) %all-gather.9.cloned.1.call-update) | async-done | bytes 9437200 | tf_op jit(solution)/shard_map/all_gather | solution.py:58
  378.7 13.4 %fusion.31 = f32[2,1024,288]{1,2,0:T(8,128)S(1)} fusion(f32[1024,2,1152]{2,0,1:T(8,128)} %all-gather.9.cloned.1.call-done, f32[2,288,1152]{2,1,0:T(8,128)S(1)} %copy-done), kind=kOutput, calls=%fused_computation.37 | convolution fusion | flops 8153726976 | bytes 14450688 | tf_op jit(solution)/shard_map/ngd,gkd->gnk/dot_general | solution.py:61
  392.1 12.7 %fusion.18 = f32[2,288,1152]{2,1,0:T(8,128)} fusion(f32[1024,2,1152]{2,0,1:T(8,128)S(1)} %copy-done.1, f32[2,288,1024]{2,1,0:T(8,128)S(1)} %copy-done.3), kind=kOutput, calls=%fused_computation.25 | convolution fusion | flops 8158445568 | bytes 14450688 | tf_op jit(solution)/shard_map/gnk,ngd->gkd/dot_general | solution.py:60
  404.8 13.8 %fusion = f32[2,288,1152]{2,1,0:T(8,128)} fusion(f32[1024,1152]{1,0:T(8,128)} %all-gather.7.cloned.1.call-done, f32[2,1024,288]{1,2,0:T(8,128)S(1)} %fusion.31, f32[2,288,1024]{2,1,0:T(8,128)S(1)} %copy-done.3), kind=kOutput, calls=%fused_computation.4 | convolution fusion | flops 8156676096 | bytes 12091392 | tf_op jit(solution)/shard_map/gnk,nd->gkd/dot_general | solution.py:62
  (28 shorter events, 6.4 us)
Async XLA Ops:
  7.2 73.2 %copy-start = (f32[2,288,1152]{2,1,0:T(8,128)S(1)}, f32[2,288,1152]{2,1,0:T(8,128)}, u32[]{:S(2)}) copy-start(f32[2,288,1152]{2,1,0:T(8,128)} %param.9) | copy-start | bytes 7962628
  7.2 59.2 %all-gather.7.cloned.1.call-start = ((), (), s32[]{:S(2)}) async-start(), calls=%async_computation.1 | async-start | bytes 4866048 | tf_op jit(solution)/shard_map/all_gather | solution.py:40
  7.9 212.0 %reduce-scatter.4.cloned.1.call-start = ((), (), s32[]{:S(2)}) async-start(), calls=%async_computation.5 | async-start | bytes 9732096
  78.9 1.4 copy-start.2
  119.4 140.3 %all-gather.11.cloned.1.call-start = ((), (), s32[]{:S(2)}) async-start(), calls=%async_computation.3 | async-start | bytes 1327104 | tf_op jit(solution)/shard_map/all_gather | solution.py:11
  223.7 43.8 %copy-start.4 = (f32[32,1152]{1,0:T(8,128)S(1)}, f32[32,1152]{1,0:T(8,128)}, u32[]{:S(2)}) copy-start(f32[32,1152]{1,0:T(8,128)} %param.7) | copy-start | bytes 442372
  224.6 81.2 %all-gather.13.cloned.1.call-start = ((), (), s32[]{:S(2)}) async-start(), calls=%async_computation.4 | async-start | bytes 1327104 | tf_op jit(solution)/shard_map/all_gather | solution.py:11
  268.5 110.2 %all-gather.9.cloned.1.call-start = ((), (), s32[]{:S(2)}) async-start(), calls=%async_computation.2 | async-start | bytes 9732096 | tf_op jit(solution)/shard_map/all_gather | solution.py:58
  378.7 13.4 %copy-start.1 = (f32[1024,2,1152]{2,0,1:T(8,128)S(1)}, f32[1024,2,1152]{2,0,1:T(8,128)}, u32[]{:S(2)}) copy-start(f32[1024,2,1152]{2,0,1:T(8,128)} %all-gather.9.cloned.1.call-done) | copy-start | bytes 28311556
  378.7 13.4 %copy-start.3 = (f32[2,288,1024]{2,1,0:T(8,128)S(1)}, f32[2,288,1024]{2,1,0:T(8,128)}, u32[]{:S(2)}) copy-start(f32[2,288,1024]{2,1,0:T(8,128)} %copy-done.2) | copy-start | bytes 7077892
Sparse Core Ops, SparseCore 0:
  10.5 55.8 all-gather.6
  119.5 100.3 reduce-scatter.3
  224.7 34.9 all-gather.10
  268.6 37.2 all-gather.12
  314.6 64.0 all-gather.8
where the time goes:
time: 430 us; the launch traced here: 425 us
  waiting for transfers between devices  282 us (66%)
  matrix products  72.2 us (17%)
  other arithmetic  30.9 us (7%)
  local copies, waits for them, and re-layouts  25.5 us (6%)
  between operations  14.1 us (3%)
    unnamed x6, waiting for transfers between devices  101 us
    all_gather x1, waiting for transfers between devices, per_device(): suffix_piece = lax.all_gather(suffix, 'feat', axis=0, tiled=True)  64.2 us
    all_gather x1, waiting for transfers between devices, per_device(): gathered = lax.all_gather(activations, 'feat', axis=0, tiled=True)  58.4 us
    all_gather x2, waiting for transfers between devices, entering(): everything = lax.all_gather(shard, axis)  58.2 us
    dot_general x1, matrix products, per_device(): jnp.einsum('gnk,gkd->ngd', feat_rows, dec_weight, precision=HIGHEST)  19.8 us
    select_n x16, other arithmetic, step(): return jnp.where(reached, new, before)  15.3 us
    unnamed x13, local copies, waits for them, and re-layouts  14.3 us
    dot_general x1, matrix products, per_device(): jnp.einsum('gnk,nd->gkd', gate, gathered, precision=HIGHEST)  13.8 us
  transfers between devices with their start and end apart: 5, of which 5 were waited for; matrix products, arithmetic and copies ran while one was open for 3% of the time, Pallas kernels for 0%

commit v1 on v0

--- a/solution.py
+++ b/solution.py
@@ -37,7 +37,9 @@
 
 def per_device(activations, enc_weight, dec_weight):
     local_groups, local_feats, model_width = enc_weight.shape
-    gathered = lax.all_gather(activations, "feat", axis=0, tiled=True)
+    gathered = jnp.concatenate(
+        lax.all_to_all(jnp.stack([activations] * lax.axis_size("feat")), "feat", 0, 0), axis=0
+    )
     tokens = gathered.shape[0]
     pre_act = jnp.einsum("nd,gkd->gnk", gathered, enc_weight, precision=HIGHEST)
     features = jax.nn.softplus(4.0 * pre_act) / 4.0

time: 430 us -> 438 us (1.019)
  blocking collectives: 0 us -> 65 us
  waiting for transfers between devices: 282 us -> 235 us
  other arithmetic: 30.9 us -> 18.9 us
    all_to_all x0 -> x1, blocking collectives: none -> 65 us  [per_device(): lax.all_to_all(jnp.stack([activations] * lax.axis_size('feat')), 'feat',...]
    all_gather x1 -> x0, waiting for transfers between devices: 58.4 us -> none  [per_device(): gathered = lax.all_gather(activations, 'feat', axis=0, tiled=True)]
    another operation x1, other arithmetic: 12.6 us -> 0.54 us  [chain_scan(): jnp.cumsum(jnp.flip(errors, 1), axis=1)]
    all_gather x2, waiting for transfers between devices: 58.2 us -> 70.2 us  [entering(): everything = lax.all_gather(shard, axis)]
    unnamed x6 -> x5, waiting for transfers between devices: 101 us -> 101 us
    unnamed x13 -> x21, local copies, waits for them, and re-layouts: 14.3 us -> 14.3 us
  transfers between devices with their start and end apart: 5 -> 4, of which waited for: 5 -> 4; matrix products, arithmetic and copies ran while one was open for 3% -> 1% of each run, Pallas kernels for 0% -> 0%
where the time goes in v1:
time: 438 us; the launch traced here: 429 us
  waiting for transfers between devices  235 us (54%)
  matrix products  68.7 us (16%)
  blocking collectives  65 us (15%)
  local copies, waits for them, and re-layouts  27.1 us (6%)
  other arithmetic  18.9 us (4%)
  between operations  14.1 us (3%)
    unnamed x5, waiting for transfers between devices  101 us
    all_gather x2, waiting for transfers between devices, entering(): everything = lax.all_gather(shard, axis)  70.2 us
    all_to_all x1, blocking collectives, per_device(): lax.all_to_all(jnp.stack([activations] * lax.axis_size('feat')), 'feat',...  65 us
    all_gather x1, waiting for transfers between devices, per_device(): suffix_piece = lax.all_gather(suffix, 'feat', axis=0, tiled=True)  64.2 us
    dot_general x1, matrix products, per_device(): jnp.einsum('gnk,gkd->ngd', feat_rows, dec_weight, precision=HIGHEST)  19.6 us
    select_n x16, other arithmetic, step(): return jnp.where(reached, new, before)  15.3 us
    unnamed x21, local copies, waits for them, and re-layouts  14.3 us
    dot_general x1, matrix products, per_device(): jnp.einsum('gnk,nd->gkd', gate, gathered, precision=HIGHEST)  13.8 us
  transfers between devices with their start and end apart: 4, of which 4 were waited for; matrix products, arithmetic and copies ran while one was open for 1% of the time, Pallas kernels for 0%

profile of v1, /device:TPU:1, one launch (start us, length us, event | category | flops | bytes accessed | tf_op | source)
XLA Modules:
  0.0 429.4 jit_solution(10685869489608518564)
XLA Ops:
  7.2 1.6 stack.2
  8.8 65.0 %all_to_all.5 = f32[32,32,1152]{2,1,0:T(8,128)S(1)} all-to-all(f32[32,32,1152]{2,1,0:T(8,128)S(1)} %stack.2), channel_id=1, replica_groups=mesh['prefix'=8,'feat'=32] {'feat'}, dimensions={0} | all-to-all | bytes 9437184 | tf_op jit(solution)/shard_map/all_to_all | solution.py:41
  73.8 9.5 %fusion.28 = f32[2,288,1024]{2,1,0:T(8,128)S(1)} fusion(f32[2,288,1152]{2,1,0:T(8,128)S(1)} %copy-done.4, f32[1024,1152,1]{1,0,2:T(8,128)S(1)} %bitcast.58), kind=kOutput, calls=%fused_computation.34 | convolution fusion | flops 8153726976 | bytes 9732096 | tf_op jit(solution)/shard_map/nd,gkd->gnk/dot_general | solution.py:44
  83.4 1.4 copy-done.1
  84.8 19.6 %convolution_bitcast_fusion = f32[1024,2,1152]{2,0,1:T(8,128)} fusion(f32[2,288,1152]{2,1,0:T(8,128)S(1)} %copy-done, f32[2,288,1024]{2,1,0:T(8,128)S(1)} %fusion.28), kind=kOutput, calls=%fused_computation.3 | convolution fusion | flops 8158445568 | bytes 14450688 | tf_op jit(solution)/shard_map/gnk,gkd->ngd/dot_general | solution.py:51
  104.3 9.6 %copy.8 = f32[1024,2,1152]{0,2,1:T(8,128)} copy(f32[1024,2,1152]{2,0,1:T(8,128)} %convolution_bitcast_fusion) | data formatting | bytes 18874368 | tf_op jit(solution)/shard_map/gnk,gkd->ngd/transpose | solution.py:51
  114.0 9.6 %copy.13 = f32[1024,2304]{1,0:T(8,128)} copy(f32[1024,2304]{0,1:T(8,128)} %bitcast.57) | data formatting | bytes 18874368
  123.7 100.5 %reduce-scatter.4.cloned.1.call-done = f32[32,2304]{1,0:T(8,128)} async-done(((f32[1024,2304]{1,0:T(8,128)}), f32[32,2304]{1,0:T(8,128)}) %reduce-scatter.4.cloned.1.call-update) | async-done | bytes 294928
  224.2 2.3 copy.14
  226.5 1.4 reduce_sum.18
  228.9 1.6 copy.10
  230.5 33.4 %all-gather.8.cloned.1.call-done = f32[256,1152]{1,0:T(8,128)} async-done(((f32[32,1152]{1,0:T(8,128)}), f32[256,1152]{1,0:T(8,128)}) %all-gather.8.cloned.1.call-update) | async-done | bytes 1179664 | tf_op jit(solution)/shard_map/all_gather | solution.py:11
  264.0 7.8 %while.30 = (s32[]{:T(128)}, f32[32,1152]{1,0:T(8,128)S(1)}, s32[]{:T(128)}, f32[8,32,1152]{2,1,0:T(8,128)}, s32[]{:T(128)}, /*index=5*/s32[]{:T(128)}) while((s32[]{:T(128)}, f32[32,1152]{1,0:T(8,128)S(1)}, s32[]{:T(128)}, f32[8,32,1152]{2,1,0:T(8,128)}, s32[]{:T(128)}, /*index=5*/s32[]{:T(128)}) %tuple.87), condition=%wide.region_3.4_spmd.clone, body=%wide.region_2.3_spmd.clone.sunk | while | flops 110596 | bytes 442461 | solution.py:20
  264.9 1.0 add_select_fusion.4
  265.9 1.0 add_select_fusion.4
  266.9 1.0 add_select_fusion.4
  267.9 1.0 add_select_fusion.4
  268.9 1.0 add_select_fusion.4
  269.8 1.0 add_select_fusion.4
  270.8 1.0 add_select_fusion.4
  273.4 36.8 %all-gather.10.cloned.1.call-done = f32[256,1152]{1,0:T(8,128)} async-done(((f32[32,1152]{1,0:T(8,128)}), f32[256,1152]{1,0:T(8,128)}) %all-gather.10.cloned.1.call-update) | async-done | bytes 1179664 | tf_op jit(solution)/shard_map/all_gather | solution.py:11
  310.1 7.9 %while.31 = (s32[]{:T(128)}, f32[32,1152]{1,0:T(8,128)S(1)}, s32[]{:T(128)}, f32[8,32,1152]{2,1,0:T(8,128)}, s32[]{:T(128)}, /*index=5*/s32[]{:T(128)}, s32[]{:T(128)}, s32[]{:T(128)}) while((s32[]{:T(128)}, f32[32,1152]{1,0:T(8,128)S(1)}, s32[]{:T(128)}, f32[8,32,1152]{2,1,0:T(8,128)}, s32[]{:T(128)}, /*index=5*/s32[]{:T(128)}, ...), condition=%wide.region_7.8_spmd.clone, body=%wide.region_6.7_spmd.clone.sunk | while | flops 110600 | bytes 442523 | solution.py:20
  311.1 1.0 add_select_fusion.5
  312.1 1.0 add_select_fusion.5
  314.1 1.0 add_select_fusion.5
  315.0 1.0 add_select_fusion.5
  316.0 1.0 add_select_fusion.5
  317.0 1.0 add_select_fusion.5
  318.7 64.2 %all-gather.6.cloned.1.call-done = f32[1024,2,1152]{2,0,1:T(8,128)} async-done(((f32[32,2,1152]{2,0,1:T(8,128)}), f32[1024,2,1152]{2,0,1:T(8,128)}) %all-gather.6.cloned.1.call-update) | async-done | bytes 9437200 | tf_op jit(solution)/shard_map/all_gather | solution.py:60
  382.9 13.0 %fusion.29 = f32[2,1024,288]{1,2,0:T(8,128)S(1)} fusion(f32[1024,2,1152]{2,0,1:T(8,128)} %all-gather.6.cloned.1.call-done, f32[2,288,1152]{2,1,0:T(8,128)S(1)} %copy-done), kind=kOutput, calls=%fused_computation.35 | convolution fusion | flops 8153726976 | bytes 14450688 | tf_op jit(solution)/shard_map/ngd,gkd->gnk/dot_general | solution.py:63
  396.0 13.8 %fusion.5 = f32[2,288,1152]{2,1,0:T(8,128)} fusion(f32[1024,1152,1]{1,0,2:T(8,128)} %bitcast.59, f32[2,1024,288]{1,2,0:T(8,128)S(1)} %fusion.29, f32[2,288,1024]{2,1,0:T(8,128)S(1)} %copy-done.2), kind=kOutput, calls=%fused_computation.13 | convolution fusion | flops 8156676096 | bytes 12091392 | tf_op jit(solution)/shard_map/gnk,nd->gkd/dot_general | solution.py:64
  409.8 12.9 %fusion.15 = f32[2,288,1152]{2,1,0:T(8,128)} fusion(f32[1024,2,1152]{2,0,1:T(8,128)S(1)} %bitcast.56, f32[2,288,1024]{2,1,0:T(8,128)S(1)} %copy-done.2), kind=kOutput, calls=%fused_computation.22 | convolution fusion | flops 8158445568 | bytes 14450688 | tf_op jit(solution)/shard_map/gnk,ngd->gkd/dot_general | solution.py:62
  (36 shorter events, 6.2 us)
Async XLA Ops:
  7.2 77.6 %copy-start = (f32[2,288,1152]{2,1,0:T(8,128)S(1)}, f32[2,288,1152]{2,1,0:T(8,128)}, u32[]{:S(2)}) copy-start(f32[2,288,1152]{2,1,0:T(8,128)} %param.9) | copy-start | bytes 7962628
  7.2 217.0 %reduce-scatter.4.cloned.1.call-start = ((), (), s32[]{:S(2)}) async-start(), calls=%async_computation.5 | async-start | bytes 9732096
  8.8 65.0 %copy-start.4 = (f32[2,288,1152]{2,1,0:T(8,128)S(1)}, f32[2,288,1152]{2,1,0:T(8,128)}, u32[]{:S(2)}) copy-start(f32[2,288,1152]{2,1,0:T(8,128)} %param.8) | copy-start | bytes 7962628
  73.8 9.5 %copy-start.3 = (f32[32,32,1152]{2,1,0:T(8,128)}, f32[32,32,1152]{2,1,0:T(8,128)S(1)}, u32[]{:S(2)}) copy-start(f32[32,32,1152]{2,1,0:T(8,128)S(1)} %all_to_all.5) | copy-start | bytes 14155780
  83.4 1.4 copy-start.1
  123.6 140.3 %all-gather.8.cloned.1.call-start = ((), (), s32[]{:S(2)}) async-start(), calls=%async_computation.3 | async-start | bytes 1327104 | tf_op jit(solution)/shard_map/all_gather | solution.py:11
  227.9 43.8 %copy-start.5 = (f32[32,1152]{1,0:T(8,128)S(1)}, f32[32,1152]{1,0:T(8,128)}, u32[]{:S(2)}) copy-start(f32[32,1152]{1,0:T(8,128)} %param.7) | copy-start | bytes 442372
  228.9 81.2 %all-gather.10.cloned.1.call-start = ((), (), s32[]{:S(2)}) async-start(), calls=%async_computation.4 | async-start | bytes 1327104 | tf_op jit(solution)/shard_map/all_gather | solution.py:11
  272.7 110.2 %all-gather.6.cloned.1.call-start = ((), (), s32[]{:S(2)}) async-start(), calls=%async_computation.2 | async-start | bytes 9732096 | tf_op jit(solution)/shard_map/all_gather | solution.py:60
  382.9 13.0 %copy-start.2 = (f32[2,288,1024]{2,1,0:T(8,128)S(1)}, f32[2,288,1024]{2,1,0:T(8,128)}, u32[]{:S(2)}) copy-start(f32[2,288,1024]{2,1,0:T(8,128)} %copy-done.1) | copy-start | bytes 7077892
  382.9 26.9 %slice-start = ((s8[9437184]{0:T(1024)(128)(4,1)}), s8[4194304]{0:T(1024)(128)(4,1)S(1)}, s32[]{:S(2)}) async-start(s8[9437184]{0:T(1024)(128)(4,1)} %bitcast.55), calls=%async_computation.6 | async-start | bytes 8388608
  382.9 26.9 %slice-start.1 = ((s8[9437184]{0:T(1024)(128)(4,1)}), s8[1048576]{0:T(1024)(128)(4,1)S(1)}, s32[]{:S(2)}) async-start(s8[9437184]{0:T(1024)(128)(4,1)} %bitcast.55), calls=%async_computation.7 | async-start | bytes 2097152
  396.0 13.8 %slice-start.2 = ((s8[9437184]{0:T(1024)(128)(4,1)}), s8[4194304]{0:T(1024)(128)(4,1)S(1)}, s32[]{:S(2)}) async-start(s8[9437184]{0:T(1024)(128)(4,1)} %bitcast.55), calls=%async_computation.8 | async-start | bytes 8388608
Sparse Core Ops, SparseCore 0:
  123.7 100.3 reduce-scatter.3
  229.0 34.9 all-gather.7
  272.8 37.2 all-gather.9
  318.9 64.0 all-gather.5
